TPU v7x, 128 devices: a whole 4x4x4 slice. The times are simulated.
128 devices in a mesh: sky: 4 (over x), exp: 32 (over z, y, core).
Axes of the slice: x: 4, y: 4, z: 4, core: 2. Of those that a mesh axis runs over, the one named last changes fastest.
Arguments:
- obs_weight: float32 [4, 32, 32, 1024], P('sky', 'exp'), may hold values from 0.25 to 4
- magnitude: float32 [4, 32, 32, 1024], P('sky', 'exp'), may hold values from -18 to 18
- star_id: int32 [4, 32, 32, 1024], P('sky', 'exp'), may hold values from 0 to 4095
- peer_count: int32 [4, 32, 32], P('sky', 'exp'), may hold values from 1 to 1024, 24576 in all within a row
- zp_index: int32 [4, 32, 32, 1024], P('sky', 'exp'), may hold values from 0 to 12095
Outputs:
- zero_points: float32 [387072], P('exp')
- residual: float32 [387072], P('exp')
Inputs may be any that keep to these rules, and one draw needn't show every extreme that they name: `peer_count`: each device's counts over the 32 owners sum to 24576, and one of them equals 1024.
All inputs are finite; a program needn't handle non-finite values.
Results may differ from a plain program's by a relative error of at most 0.0003.
Values sent between devices are 32-bit elements; how exact they have to be, the bound alone decides.
A program may use at most 64 MiB of HBM per device.

v0:
```python
import math

import jax
import jax.numpy as jnp
from jax import lax
from jax.sharding import PartitionSpec as P

CAP = 1024
STAR_DEV = 4096
ITERS = 2
ZP_DEV = 12096


ridge = 1.0
prior = 1.0
exact = lax.Precision.HIGHEST


def from_everyone(x, axis):
    copies = jnp.broadcast_to(x, (lax.axis_size(axis), *x.shape))
    return lax.all_to_all(copies, axis, split_axis=0, concat_axis=0, tiled=True)


def over_copies(x, axis):
    everything = from_everyone(x, axis)
    return jnp.sum(everything, axis=0)


def together(arrays, axis):
    ends = [0]
    for a in arrays:
        ends.append(ends[-1] + a.size)
    so_far = over_copies(jnp.concatenate([a.ravel() for a in arrays]), axis)
    return tuple((so_far[b:e].reshape(a.shape) for a, b, e in zip(arrays, ends, ends[1:])))


def hot_parts(index, size):
    rows = (size + 127) // 128
    high = (index[:, None] // 128 == jnp.arange(rows, dtype=jnp.int32)[None, :]).astype(jnp.float32)
    low = (index[:, None] % 128 == jnp.arange(128, dtype=jnp.int32)[None, :]).astype(jnp.float32)
    return (high, low)


def sum_by(values, index, size):
    total = values.shape[0]
    block = math.gcd(total, 2048)
    count = total // block

    def sum_one_block(pair):
        high, low = hot_parts(pair[1], size)
        return jnp.einsum("sh,sl->hl", high, low * pair[0][:, None], precision=exact)

    parts = lax.map(sum_one_block, (values.reshape(count, block), index.reshape(count, block)))
    return jnp.sum(parts, axis=0).reshape(-1)[:size]


def take_by(field, index):
    size = field.shape[0]
    rows = (size + 127) // 128
    table = jnp.pad(field, (0, rows * 128 - size)).reshape(rows, 128)
    total = index.shape[0]
    block = math.gcd(total, 2048)
    count = total // block

    def take_one_block(piece):
        high, low = hot_parts(piece, size)
        picked = jnp.dot(high, table, precision=exact)
        return jnp.sum(picked * low, axis=1)

    return lax.map(take_one_block, index.reshape(count, block)).reshape(-1)


def body(obs_weight, magnitude, star_id, peer_count, zp_index):
    n_exp = lax.axis_size("exp")
    slots = jnp.arange(CAP, dtype=jnp.int32)
    live = (slots[None, :] < peer_count[0, 0][:, None]).astype(jnp.float32)
    weight = (obs_weight[0, 0] * live).reshape(-1)
    stars = star_id[0, 0].reshape(-1)
    wsum = prior + sum_by(weight, stars, STAR_DEV)
    owned = zp_index[0, 0]
    owned_flat = owned.reshape(-1)

    def reduce_slots(values):
        flat = values.reshape(-1)
        mean = sum_by(weight * flat, stars, STAR_DEV) / wsum
        term = (weight * (flat - take_by(mean, stars))).reshape(n_exp, CAP)
        arrived = lax.all_to_all(term, "exp", split_axis=0, concat_axis=0, tiled=True)
        partial_sum = sum_by(arrived.reshape(-1), owned_flat, ZP_DEV)
        return over_copies(partial_sum, "sky")

    def slot_values(field):
        picked = take_by(field, owned_flat).reshape(n_exp, CAP)
        return lax.all_to_all(picked, "exp", split_axis=0, concat_axis=0, tiled=True)

    def operate(field):
        return reduce_slots(slot_values(field)) + ridge * field

    right = reduce_slots(magnitude[0, 0])
    zero_points = jnp.zeros_like(right)
    residual = right

    def paired(vector, image):
        return together((jnp.sum(vector * vector), jnp.sum(vector * image)), "exp")

    image = operate(residual)
    norm_now, product = paired(residual, image)
    alpha = norm_now / product
    direction = residual
    along = image
    for step in range(ITERS):
        zero_points = zero_points + alpha * direction
        residual = residual - alpha * along
        if step + 1 < ITERS:
            image = operate(residual)
            norm_next, product = paired(residual, image)
            ratio = norm_next / norm_now
            alpha = norm_next / (product - ratio * norm_next / alpha)
            direction = residual + ratio * direction
            along = image + ratio * along
            norm_now = norm_next
    return (zero_points, residual)


def solution(mesh):
    return jax.shard_map(
        body,
        mesh=mesh,
        in_specs=(
            P("sky", "exp", None, None),
            P("sky", "exp", None, None),
            P("sky", "exp", None, None),
            P("sky", "exp", None),
            P("sky", "exp", None, None),
        ),
        out_specs=(P("exp"), P("exp")),
        check_vma=False,
    )
```

profile of v0, /device:TPU:1, one launch (start us, length us, event | category | flops | bytes accessed | tf_op | source)
XLA Modules:
  0.0 474.8 jit_solution(758452459960001158)
XLA Ops:
  5.0 30.9 %while.145 = (s32[]{:T(128)}, f32[16,32,128]{2,1,0:T(8,128)S(1)}, s32[16,2048]{1,0:T(8,128)S(1)}, f32[16,2048]{1,0:T(8,128)S(1)}, s32[]{:T(128)}) while((s32[]{:T(128)}, f32[16,32,128]{2,1,0:T(8,128)S(1)}, s32[16,2048]{1,0:T(8,128)S(1)}, f32[16,2048]{1,0:T(8,128)S(1)}, s32[]{:T(128)}) %tuple.308), condition=%wide.region_4.5_spmd, body=%wide.region_3.4_spmd.sunk | while | flops 101292032 | bytes 98377 | solution.py:53
  35.9 30.9 %while.144 = (s32[]{:T(128)}, f32[16,32,128]{2,1,0:T(8,128)S(1)}, s32[16,2048]{1,0:T(8,128)S(1)}, f32[16,2048]{1,0:T(8,128)S(1)}, s32[]{:T(128)}) while((s32[]{:T(128)}, f32[16,32,128]{2,1,0:T(8,128)S(1)}, s32[16,2048]{1,0:T(8,128)S(1)}, f32[16,2048]{1,0:T(8,128)S(1)}, s32[]{:T(128)}) %tuple.341), condition=%wide.region_1.2_spmd, body=%wide.region_0.1_spmd.sunk | while | flops 101292032 | bytes 98377 | solution.py:53
  66.9 23.0 %while.146 = (s32[]{:T(128)}, f32[16,2048]{1,0:T(8,128)S(1)}, s32[16,2048]{1,0:T(8,128)S(1)}, f32[32,128]{1,0:T(8,128)S(1)}, s32[]{:T(128)}, /*index=5*/s32[]{:T(128)}) while((s32[]{:T(128)}, f32[16,2048]{1,0:T(8,128)S(1)}, s32[16,2048]{1,0:T(8,128)S(1)}, f32[32,128]{1,0:T(8,128)S(1)}, s32[]{:T(128)}, /*index=5*/s32[]{:T(128)}) %tuple.342), condition=%wide.region_8.9_spmd, body=%wide.region_6.8_spmd.sunk | while | flops 101552128 | bytes 98381 | solution.py:70
  91.0 9.7 %all-to-all-start = ((f32[32,1,1024]{2,1,0:T(1,128)}), f32[32,1,1024]{2,1,0:T(1,128)S(1)}, u32[]{:S(2)}, u32[]{:S(2)}) async-start(f32[32,1,1024]{2,1,0:T(1,128)} %subtract_multiply_fusion.2), calls=%async_computation | async-start | bytes 262144 | tf_op jit(solution)/shard_map/all_to_all | solution.py:87
  100.8 7.6 %all-to-all-done = f32[32,1,1024]{2,1,0:T(1,128)S(1)} async-done(((f32[32,1,1024]{2,1,0:T(1,128)}), f32[32,1,1024]{2,1,0:T(1,128)S(1)}, u32[]{:S(2)}, u32[]{:S(2)}) %all-to-all-start) | async-done | bytes 131104 | tf_op jit(solution)/shard_map/all_to_all | solution.py:87
  108.8 31.6 %while.147 = (s32[]{:T(128)}, f32[16,95,128]{2,1,0:T(8,128)S(1)}, s32[16,2048]{1,0:T(8,128)S(1)}, f32[16,2048]{1,0:T(8,128)S(1)}, s32[]{:T(128)}) while((s32[]{:T(128)}, f32[16,95,128]{2,1,0:T(8,128)S(1)}, s32[16,2048]{1,0:T(8,128)S(1)}, f32[16,2048]{1,0:T(8,128)S(1)}, s32[]{:T(128)}) %tuple.314), condition=%wide.region_10.11_spmd, body=%wide.region_9.10_spmd.sunk | while | flops 299601920 | bytes 131145 | solution.py:53
  108.9 1.9 fusion.122
  110.8 1.9 fusion.122
  112.8 1.9 fusion.122
  114.8 1.9 fusion.122
  116.8 1.9 fusion.122
  120.7 1.9 fusion.122
  122.7 1.9 fusion.122
  124.7 1.9 fusion.122
  126.6 1.9 fusion.122
  128.6 1.9 fusion.122
  134.5 1.9 fusion.122
  136.5 1.9 fusion.122
  138.5 1.9 fusion.122
  141.2 4.0 all-to-all-start.1
  145.2 5.2 %all-to-all-done.1 = f32[4,1,12096]{2,1,0:T(1,128)S(1)} async-done(((f32[4,1,12096]{2,1,0:T(1,128)}), f32[4,1,12096]{2,1,0:T(1,128)S(1)}, u32[]{:S(2)}, u32[]{:S(2)}) %all-to-all-start.1) | async-done | bytes 193568 | tf_op jit(solution)/shard_map/all_to_all | solution.py:21
  150.6 23.9 %while.148 = (s32[]{:T(128)}, f32[16,2048]{1,0:T(8,128)S(1)}, s32[16,2048]{1,0:T(8,128)S(1)}, f32[95,128]{1,0:T(8,128)S(1)}, s32[]{:T(128)}, /*index=5*/s32[]{:T(128)}) while((s32[]{:T(128)}, f32[16,2048]{1,0:T(8,128)S(1)}, s32[16,2048]{1,0:T(8,128)S(1)}, f32[95,128]{1,0:T(8,128)S(1)}, s32[]{:T(128)}, /*index=5*/s32[]{:T(128)}) %tuple.347), condition=%wide.region_16.17_spmd, body=%wide.region_14.16_spmd.sunk | while | flops 299862016 | bytes 130637 | solution.py:70
  175.4 5.3 %all-to-all-start.2 = ((f32[32,1,1024]{2,1,0:T(1,128)}), f32[32,1,1024]{2,1,0:T(1,128)S(1)}, u32[]{:S(2)}, u32[]{:S(2)}) async-start(f32[32,1,1024]{2,1,0:T(1,128)} %all_to_all.46), calls=%async_computation.2 | async-start | bytes 262144 | tf_op jit(solution)/shard_map/all_to_all | solution.py:93
  180.7 7.7 %all-to-all-done.2 = f32[32,1,1024]{2,1,0:T(1,128)S(1)} async-done(((f32[32,1,1024]{2,1,0:T(1,128)}), f32[32,1,1024]{2,1,0:T(1,128)S(1)}, u32[]{:S(2)}, u32[]{:S(2)}) %all-to-all-start.2) | async-done | bytes 131104 | tf_op jit(solution)/shard_map/all_to_all | solution.py:93
  188.9 30.9 %while.149 = (s32[]{:T(128)}, f32[16,32,128]{2,1,0:T(8,128)S(1)}, s32[16,2048]{1,0:T(8,128)S(1)}, f32[16,2048]{1,0:T(8,128)S(1)}, s32[]{:T(128)}) while((s32[]{:T(128)}, f32[16,32,128]{2,1,0:T(8,128)S(1)}, s32[16,2048]{1,0:T(8,128)S(1)}, f32[16,2048]{1,0:T(8,128)S(1)}, s32[]{:T(128)}) %tuple.343), condition=%wide.region_18.19_spmd, body=%wide.region_17.18_spmd.sunk | while | flops 101292032 | bytes 98377 | solution.py:53
  219.8 23.0 %while.150 = (s32[]{:T(128)}, f32[16,2048]{1,0:T(8,128)S(1)}, s32[16,2048]{1,0:T(8,128)S(1)}, f32[32,128]{1,0:T(8,128)S(1)}, s32[]{:T(128)}, /*index=5*/s32[]{:T(128)}) while((s32[]{:T(128)}, f32[16,2048]{1,0:T(8,128)S(1)}, s32[16,2048]{1,0:T(8,128)S(1)}, f32[32,128]{1,0:T(8,128)S(1)}, s32[]{:T(128)}, /*index=5*/s32[]{:T(128)}) %tuple.344), condition=%wide.region_22.23_spmd, body=%wide.region_20.22_spmd.sunk | while | flops 101552128 | bytes 98381 | solution.py:70
  243.9 3.9 all-to-all-start.3
  247.8 7.7 %all-to-all-done.3 = f32[32,1,1024]{2,1,0:T(1,128)S(1)} async-done(((f32[32,1,1024]{2,1,0:T(1,128)}), f32[32,1,1024]{2,1,0:T(1,128)S(1)}, u32[]{:S(2)}, u32[]{:S(2)}) %all-to-all-start.3) | async-done | bytes 131104 | tf_op jit(solution)/shard_map/all_to_all | solution.py:87
  256.0 31.6 %while.151 = (s32[]{:T(128)}, f32[16,95,128]{2,1,0:T(8,128)S(1)}, s32[16,2048]{1,0:T(8,128)S(1)}, f32[16,2048]{1,0:T(8,128)S(1)}, s32[]{:T(128)}) while((s32[]{:T(128)}, f32[16,95,128]{2,1,0:T(8,128)S(1)}, s32[16,2048]{1,0:T(8,128)S(1)}, f32[16,2048]{1,0:T(8,128)S(1)}, s32[]{:T(128)}) %tuple.348), condition=%wide.region_24.25_spmd, body=%wide.region_23.24_spmd.sunk | while | flops 299601920 | bytes 131145 | solution.py:53
  287.8 7.7 %all_to_all.66 = f32[4,1,12096]{2,1,0:T(1,128)S(1)} all-to-all(f32[4,1,12096]{2,1,0:T(1,128)S(1)} %broadcast_in_dim.171), channel_id=1, replica_groups=mesh['sky'=4,'exp'=32] {'sky'}, dimensions={0} | all-to-all | bytes 387072 | tf_op jit(solution)/shard_map/all_to_all | solution.py:21
  298.4 5.0 %all-to-all-start.5 = ((f32[32,1,2]{2,1,0:T(1,128)}), f32[32,1,2]{2,1,0:T(1,128)S(1)}, u32[]{:S(2)}, u32[]{:S(2)}) async-start(f32[32,1,2]{2,1,0:T(1,128)} %broadcast_in_dim.172), calls=%async_computation.5 | async-start | bytes 32768 | tf_op jit(solution)/shard_map/all_to_all | solution.py:21
  303.4 7.0 %all-to-all-done.5 = f32[32,1,2]{2,1,0:T(1,128)S(1)} async-done(((f32[32,1,2]{2,1,0:T(1,128)}), f32[32,1,2]{2,1,0:T(1,128)S(1)}, u32[]{:S(2)}, u32[]{:S(2)}) %all-to-all-start.5) | async-done | bytes 288 | tf_op jit(solution)/shard_map/all_to_all | solution.py:21
  312.3 23.9 %while.152 = (s32[]{:T(128)}, f32[16,2048]{1,0:T(8,128)S(1)}, s32[16,2048]{1,0:T(8,128)S(1)}, f32[95,128]{1,0:T(8,128)S(1)}, s32[]{:T(128)}, /*index=5*/s32[]{:T(128)}) while((s32[]{:T(128)}, f32[16,2048]{1,0:T(8,128)S(1)}, s32[16,2048]{1,0:T(8,128)S(1)}, f32[95,128]{1,0:T(8,128)S(1)}, s32[]{:T(128)}, /*index=5*/s32[]{:T(128)}) %tuple.349), condition=%wide.region_32.33_spmd, body=%wide.region_30.32_spmd.sunk | while | flops 299862016 | bytes 130637 | solution.py:70
  337.1 4.2 all-to-all-start.6
  341.2 7.7 %all-to-all-done.6 = f32[32,1,1024]{2,1,0:T(1,128)S(1)} async-done(((f32[32,1,1024]{2,1,0:T(1,128)}), f32[32,1,1024]{2,1,0:T(1,128)S(1)}, u32[]{:S(2)}, u32[]{:S(2)}) %all-to-all-start.6) | async-done | bytes 131104 | tf_op jit(solution)/shard_map/all_to_all | solution.py:93
  349.4 30.9 %while.153 = (s32[]{:T(128)}, f32[16,32,128]{2,1,0:T(8,128)S(1)}, s32[16,2048]{1,0:T(8,128)S(1)}, f32[16,2048]{1,0:T(8,128)S(1)}, s32[]{:T(128)}) while((s32[]{:T(128)}, f32[16,32,128]{2,1,0:T(8,128)S(1)}, s32[16,2048]{1,0:T(8,128)S(1)}, f32[16,2048]{1,0:T(8,128)S(1)}, s32[]{:T(128)}) %tuple.345), condition=%wide.region_34.35_spmd, body=%wide.region_33.34_spmd.sunk | while | flops 101292032 | bytes 98377 | solution.py:53
  380.3 23.0 %while.154 = (s32[]{:T(128)}, f32[16,2048]{1,0:T(8,128)S(1)}, s32[16,2048]{1,0:T(8,128)S(1)}, f32[32,128]{1,0:T(8,128)S(1)}, s32[]{:T(128)}, /*index=5*/s32[]{:T(128)}) while((s32[]{:T(128)}, f32[16,2048]{1,0:T(8,128)S(1)}, s32[16,2048]{1,0:T(8,128)S(1)}, f32[32,128]{1,0:T(8,128)S(1)}, s32[]{:T(128)}, /*index=5*/s32[]{:T(128)}) %tuple.346), condition=%wide.region_38.39_spmd, body=%wide.region_36.38_spmd.sunk | while | flops 101552128 | bytes 98381 | solution.py:70
  403.8 11.3 %all_to_all.67 = f32[32,1,1024]{2,1,0:T(1,128)S(1)} all-to-all(f32[32,1,1024]{2,1,0:T(1,128)S(1)} %subtract_multiply_fusion), channel_id=1, replica_groups=mesh['sky'=4,'exp'=32] {'exp'}, dimensions={0} | all-to-all | bytes 262144 | tf_op jit(solution)/shard_map/all_to_all | solution.py:87
  415.5 31.6 %while.155 = (s32[]{:T(128)}, f32[16,95,128]{2,1,0:T(8,128)S(1)}, s32[16,2048]{1,0:T(8,128)S(1)}, f32[16,2048]{1,0:T(8,128)S(1)}, s32[]{:T(128)}) while((s32[]{:T(128)}, f32[16,95,128]{2,1,0:T(8,128)S(1)}, s32[16,2048]{1,0:T(8,128)S(1)}, f32[16,2048]{1,0:T(8,128)S(1)}, s32[]{:T(128)}) %tuple.350), condition=%wide.region_40.41_spmd, body=%wide.region_39.40_spmd.sunk | while | flops 299601920 | bytes 131145 | solution.py:53
  415.6 1.9 fusion.138
  417.6 1.9 fusion.138
  423.5 1.9 fusion.138
  425.5 1.9 fusion.138
  427.4 1.9 fusion.138
  437.3 1.9 fusion.138
  443.2 1.9 fusion.138
  447.3 7.7 %all_to_all.68 = f32[4,1,12096]{2,1,0:T(1,128)S(1)} all-to-all(f32[4,1,12096]{2,1,0:T(1,128)S(1)} %broadcast_in_dim.173), channel_id=1, replica_groups=mesh['sky'=4,'exp'=32] {'sky'}, dimensions={0} | all-to-all | bytes 387072 | tf_op jit(solution)/shard_map/all_to_all | solution.py:21
  457.3 11.6 %all_to_all.69 = f32[32,1,2]{2,1,0:T(1,128)S(1)} all-to-all(f32[32,1,2]{2,1,0:T(1,128)S(1)} %broadcast_in_dim.174), channel_id=1, replica_groups=mesh['sky'=4,'exp'=32] {'exp'}, dimensions={0} | all-to-all | bytes 512 | tf_op jit(solution)/shard_map/all_to_all | solution.py:21
  (832 shorter events, 309.1 us)
Async XLA Ops:
  0.6 0.7 copy-start.4
  2.2 0.9 copy-start.1
  3.1 0.9 copy-start
  4.0 0.9 copy-start.2
  91.0 9.7 %copy-start.3 = (s32[1,1,32,1024]{3,2,1,0:T(8,128)S(1)}, s32[1,1,32,1024]{3,2,1,0:T(8,128)}, u32[]{:S(2)}) copy-start(s32[1,1,32,1024]{3,2,1,0:T(8,128)} %param.33) | copy-start | bytes 393220
  91.0 17.4 %all-to-all-start = ((f32[32,1,1024]{2,1,0:T(1,128)}), f32[32,1,1024]{2,1,0:T(1,128)S(1)}, u32[]{:S(2)}, u32[]{:S(2)}) async-start(f32[32,1,1024]{2,1,0:T(1,128)} %subtract_multiply_fusion.2), calls=%async_computation | async-start | bytes 262144 | tf_op jit(solution)/shard_map/all_to_all | solution.py:87
  141.2 9.2 %all-to-all-start.1 = ((f32[4,1,12096]{2,1,0:T(1,128)}), f32[4,1,12096]{2,1,0:T(1,128)S(1)}, u32[]{:S(2)}, u32[]{:S(2)}) async-start(f32[4,1,12096]{2,1,0:T(1,128)} %broadcast_in_dim.170), calls=%async_computation.1 | async-start | bytes 389120 | tf_op jit(solution)/shard_map/all_to_all | solution.py:21
  175.4 13.1 %all-to-all-start.2 = ((f32[32,1,1024]{2,1,0:T(1,128)}), f32[32,1,1024]{2,1,0:T(1,128)S(1)}, u32[]{:S(2)}, u32[]{:S(2)}) async-start(f32[32,1,1024]{2,1,0:T(1,128)} %all_to_all.46), calls=%async_computation.2 | async-start | bytes 262144 | tf_op jit(solution)/shard_map/all_to_all | solution.py:93
  243.9 11.7 %all-to-all-start.3 = ((f32[32,1,1024]{2,1,0:T(1,128)}), f32[32,1,1024]{2,1,0:T(1,128)S(1)}, u32[]{:S(2)}, u32[]{:S(2)}) async-start(f32[32,1,1024]{2,1,0:T(1,128)} %subtract_multiply_fusion.1), calls=%async_computation.3 | async-start | bytes 262144 | tf_op jit(solution)/shard_map/all_to_all | solution.py:87
  298.4 12.0 %all-to-all-start.5 = ((f32[32,1,2]{2,1,0:T(1,128)}), f32[32,1,2]{2,1,0:T(1,128)S(1)}, u32[]{:S(2)}, u32[]{:S(2)}) async-start(f32[32,1,2]{2,1,0:T(1,128)} %broadcast_in_dim.172), calls=%async_computation.5 | async-start | bytes 32768 | tf_op jit(solution)/shard_map/all_to_all | solution.py:21
  337.1 11.9 %all-to-all-start.6 = ((f32[32,1,1024]{2,1,0:T(1,128)}), f32[32,1,1024]{2,1,0:T(1,128)S(1)}, u32[]{:S(2)}, u32[]{:S(2)}) async-start(f32[32,1,1024]{2,1,0:T(1,128)} %all_to_all.51), calls=%async_computation.6 | async-start | bytes 262144 | tf_op jit(solution)/shard_map/all_to_all | solution.py:93
where the time goes:
time: 476 us; the launch traced here: 475 us
  matrix products  304 us (64%)
  waiting for transfers between devices  42.9 us (9%)
  blocking collectives  38.3 us (8%)
  starting transfers between devices  32.2 us (7%)
  local copies, waits for them, and re-layouts  30.1 us (6%)
  other arithmetic  12.6 us (3%)
  loops' own time  7.56 us (2%)
  between operations  6.95 us (1%)
    dot_general x112, matrix products, sum_one_block(): jnp.einsum('sh,sl->hl', high, low * pair[0][:, None], precision=exact)  210 us
    dot_general x80, matrix products, take_one_block(): picked = jnp.dot(high, table, precision=exact)  94.7 us
    all_to_all x3, blocking collectives, from_everyone(): return lax.all_to_all(copies, axis, split_axis=0, concat_axis=0, tiled=True)  27 us
    dynamic_update_slice x80, local copies, waits for them, and re-layouts, take_by(): return lax.map(take_one_block, index.reshape(count, block)).reshape(-1)  16.4 us
    all_to_all x2, waiting for transfers between devices, slot_values(): lax.all_to_all(picked, 'exp', split_axis=0, concat_axis=0, tiled=True)  15.5 us
    all_to_all x2, waiting for transfers between devices, reduce_slots(): lax.all_to_all(term, 'exp', split_axis=0, concat_axis=0, tiled=True)  15.3 us
    all_to_all x2, starting transfers between devices, reduce_slots(): lax.all_to_all(term, 'exp', split_axis=0, concat_axis=0, tiled=True)  13.6 us
    all_to_all x2, waiting for transfers between devices, from_everyone(): return lax.all_to_all(copies, axis, split_axis=0, concat_axis=0, tiled=True)  12.2 us
  transfers between devices with their start and end apart: 6, of which 6 were waited for; matrix products, arithmetic and copies ran while one was open for 0% of the time, Pallas kernels for 0%

commit v1 on v0

v1 whole, which is shorter than its diff:
```python
import functools

import jax
import jax.numpy as jnp
from jax import lax
from jax.experimental import pallas as pl
from jax.experimental.pallas import tpu as pltpu
from jax.sharding import PartitionSpec as P

CAP = 1024
STAR_DEV = 4096
ZP_DEV = 12096
LANES = 128
SUB = CAP // LANES
STAR_ROWS = STAR_DEV // LANES
ZP_ROWS = (ZP_DEV + LANES - 1) // LANES
ZP_PAD = 96
PLANE = 8

ridge = 1.0
prior = 1.0
f32 = jnp.float32
bf16 = jnp.bfloat16
NT = (((1,), (1,)), ((), ()))
MESH = pl.DeviceIdType.MESH


def two_parts(x):
    coarse = x.astype(bf16)
    return coarse, (x - coarse.astype(f32)).astype(bf16)


def as_code(x):
    return x.astype(f32).astype(bf16)


def row_of(x, r, n):
    return jnp.broadcast_to(x[r : r + 1, :], (n, LANES))


def scatter(high, low, parts, n_high, n_low):
    rows = high.shape[0]
    iota_high = as_code(lax.broadcasted_iota(jnp.int32, (n_high, LANES), 0))
    iota_low = as_code(lax.broadcasted_iota(jnp.int32, (n_low, LANES), 0))
    one, zero = jnp.ones((), bf16), jnp.zeros((), bf16)
    hot, weighted = [], [[] for _ in parts]
    for r in range(rows):
        hot.append(jnp.where(row_of(high, r, n_high) == iota_high, one, zero))
        mask = row_of(low, r, n_low) == iota_low
        for column, part in zip(weighted, parts):
            column.append(jnp.where(mask, row_of(part, r, n_low), zero))
    hot = jnp.concatenate(hot, axis=1)
    weighted = jnp.concatenate([jnp.concatenate(c, axis=1) for c in weighted], axis=0)
    return lax.dot_general(hot, weighted, NT, preferred_element_type=f32)


def pick(table, rows, index):
    high, low = lax.shift_right_logical(index, 7), index & 127
    found = jnp.zeros(index.shape, f32)
    for r in range(rows):
        line = jnp.broadcast_to(table[r : r + 1, :], index.shape)
        found = jnp.where(high == r, jnp.take_along_axis(line, low, axis=1), found)
    return found


def star_codes(index):
    high = lax.shift_right_logical(index, 7) + STAR_ROWS * (lax.shift_right_logical(index, 5) & 3)
    return as_code(high), as_code(index & 31)


def zp_codes(index):
    high = lax.shift_right_logical(index, 7) + ZP_PAD * (lax.shift_right_logical(index, 6) & 1)
    return as_code(high), as_code(index & 63)


def star_table(pair):
    both = pair[:, :32] + pair[:, 32:64]
    return jnp.concatenate([both[32 * q : 32 * q + 32, :] for q in range(4)], axis=1)


def kernel(
    n_sky, n_exp,
    count, weight_in, magnitude_in, star_in, zp_in,
    x_out, r_out,
    weight, magnitude, star, zp, wsum, mean, field, image, image2,
    sent, got, shares, dots, loads, sends, arrivals,
):
    sky, me = lax.axis_index("sky"), lax.axis_index("exp")
    my_z, my_y, my_c = me // 8, (me // 2) % 4, me % 2
    planes = n_exp // PLANE

    incoming = []
    for a, (source, target) in enumerate(((weight_in, weight), (magnitude_in, magnitude), (star_in, star), (zp_in, zp))):
        for c in range(SUB):
            copy = pltpu.make_async_copy(
                source.at[0, 0, :, pl.ds(c * LANES, LANES)], target.at[:, c, :], loads.at[a, c])
            copy.start()
            incoming.append(copy)

    barrier = pltpu.get_barrier_semaphore()

    @pl.loop(1, n_exp)
    def _(t):
        pl.semaphore_signal(barrier, inc=1, device_id={"exp": lax.rem(me + t, n_exp)}, device_id_type=MESH)

    for t in range(1, n_sky):
        pl.semaphore_signal(barrier, inc=1, device_id={"sky": lax.rem(sky + t, n_sky)}, device_id_type=MESH)

    for copy in incoming:
        copy.wait()

    slot = lax.broadcasted_iota(jnp.int32, (SUB, LANES), 0) * LANES + lax.broadcasted_iota(jnp.int32, (SUB, LANES), 1)

    @pl.loop(0, n_exp)
    def _(j):
        weight[j] = jnp.where(slot < count[0, 0, j], weight[j], 0.0)

    def flat(x):
        return x.reshape(PLANE * SUB, LANES)

    def plane(ref, base):
        return flat(ref[pl.ds(base, PLANE)])

    def first(g, total):
        base = pl.multiple_of(g * PLANE, PLANE)
        w = plane(weight, base)
        high, low = star_codes(plane(star, base))
        return total + scatter(high, low, two_parts(w) + two_parts(w * plane(magnitude, base)), 128, 32)

    total = lax.fori_loop(0, planes, first, jnp.zeros((128, 128), f32))
    wsum[...] = prior + star_table(total[:, :64])
    mean[...] = star_table(total[:, 64:]) / wsum[...]

    pl.semaphore_wait(barrier, n_exp - 1 + n_sky - 1)

    def exchange(phase, block):
        def send(j, step):
            pltpu.make_async_remote_copy(
                src_ref=sent.at[phase, j], dst_ref=got.at[phase, me],
                send_sem=sends.at[phase], recv_sem=arrivals.at[phase, step],
                device_id={"exp": j}, device_id_type=MESH).start()

        def plane_of(step, last):
            z = lax.rem(my_z + (planes - 1 - step), planes)
            spots = [(dy, dc) for dy in (2, 1, 3, 0) for dc in (1, 0)]
            before = None
            for dy, dc in spots:
                j = z * 8 + lax.rem(my_y + dy, 4) * 2 + lax.rem(my_c + dc, 2)
                if last and (dy, dc) == (0, 0):
                    got[phase, me] = block(me)
                else:
                    sent[phase, j] = block(j)
                if before is not None:
                    send(before, step)
                before = None if last and (dy, dc) == (0, 0) else j
            if before is not None:
                send(before, step)

        @pl.loop(0, planes - 1)
        def _(step):
            plane_of(step, False)

        plane_of(planes - 1, True)

    def arrive(phase, step, blocks):
        pltpu.make_async_copy(
            sent.at[phase, pl.ds(0, blocks)], got.at[phase, pl.ds(0, blocks)], arrivals.at[phase, step]).wait()

    def over_planes(phase, shape, part):
        def one(step, total):
            arrive(phase, step, PLANE)
            return total + part(pl.multiple_of(lax.rem(my_z + 1 + step, planes) * PLANE, PLANE))

        total = lax.fori_loop(0, planes - 1, one, jnp.zeros(shape, f32))
        arrive(phase, planes - 1, PLANE - 1)
        return total + part(pl.multiple_of(my_z * PLANE, PLANE))

    def to_owners(phase, values):
        exchange(phase, lambda j: weight[j] * (values(j) - pick(mean, STAR_ROWS, star[j])))

    def from_owners(phase, source):
        exchange(phase, lambda k: pick(source, ZP_ROWS, zp[k]))

    def star_means(phase):
        def part(base):
            high, low = star_codes(plane(star, base))
            return scatter(high, low, two_parts(plane(weight, base) * flat(got[phase, pl.ds(base, PLANE)])), 128, 32)

        mean[...] = star_table(over_planes(phase, (128, 64), part)) / wsum[...]

    def owner_sums(phase, turn):
        def part(base):
            high, low = zp_codes(plane(zp, base))
            return scatter(high, low, two_parts(flat(got[phase, pl.ds(base, PLANE)])), 2 * ZP_PAD, 64)

        pair = over_planes(phase, (2 * ZP_PAD, 128), part)
        both = pair + pltpu.roll(pair, 64, 1)
        lane = lax.broadcasted_iota(jnp.int32, (ZP_PAD, LANES), 1)
        shares[turn, sky] = jnp.where(lane < 64, both[:ZP_PAD], both[ZP_PAD:])
        for t in (2, 1, 3):
            pltpu.make_async_remote_copy(
                src_ref=shares.at[turn, sky], dst_ref=shares.at[turn, sky],
                send_sem=sends.at[5 + turn], recv_sem=arrivals.at[5 + turn, 0],
                device_id={"sky": lax.rem(sky + t, n_sky)}, device_id_type=MESH).start()
        pltpu.make_async_copy(
            shares.at[turn, pl.ds(0, 3)], shares.at[turn, pl.ds(0, 3)], arrivals.at[5 + turn, 0]).wait()
        return (shares[turn, 0] + shares[turn, 1]) + (shares[turn, 2] + shares[turn, 3])

    def put_dots(turn, pairs):
        rows = [jnp.sum(a * b, axis=0, keepdims=True) for a, b in pairs]
        rows += [jnp.zeros((1, LANES), f32)] * (SUB - len(rows))
        dots[turn, me] = jnp.concatenate(rows, axis=0)

        @pl.loop(1, n_exp)
        def _(t):
            pltpu.make_async_remote_copy(
                src_ref=dots.at[turn, me], dst_ref=dots.at[turn, me],
                send_sem=sends.at[8 + turn], recv_sem=arrivals.at[8 + turn, 0],
                device_id={"exp": lax.rem(me + n_exp - t, n_exp)}, device_id_type=MESH).start()

    def take_dots(turn):
        pltpu.make_async_copy(
            dots.at[turn, pl.ds(0, n_exp - 1)], dots.at[turn, pl.ds(0, n_exp - 1)], arrivals.at[8 + turn, 0]).wait()
        return jnp.sum(jnp.sum(dots[turn], axis=0), axis=1, keepdims=True)

    to_owners(0, lambda j: magnitude[j])
    field[...] = owner_sums(0, 0)
    from_owners(1, field)
    star_means(1)
    to_owners(2, lambda j: got[1, j])
    image[...] = owner_sums(2, 1) + ridge * field[...]
    put_dots(0, ((field[...], field[...]), (field[...], image[...])))
    from_owners(3, image)
    star_means(3)
    to_owners(4, lambda j: got[3, j])
    image2[...] = owner_sums(4, 2) + ridge * image[...]

    def whole(x):
        return jnp.broadcast_to(jnp.broadcast_to(x, (1, LANES)), (ZP_PAD, LANES))

    b, c, d = field[...], image[...], image2[...]
    sums = take_dots(0)
    norm_now = sums[0:1]
    alpha = norm_now / sums[1:2]
    residual = b - whole(alpha) * c
    along = c - whole(alpha) * d
    put_dots(1, ((residual, residual), (residual, along), (residual, c), (b, along)))
    later = take_dots(1)
    norm_next = later[0:1]
    ratio = norm_next / norm_now
    curve = later[1:2] + ratio * (later[2:3] + later[3:4]) + ratio * ratio * sums[1:2]
    step = norm_next / curve
    x_out[...] = whole(alpha) * b + whole(step) * (residual + whole(ratio) * b)
    r_out[...] = residual - whole(step) * (along + whole(ratio) * c)

    for phase in range(5):
        pltpu.make_async_copy(
            sent.at[phase, pl.ds(0, n_exp - 1)], got.at[phase, pl.ds(0, n_exp - 1)], sends.at[phase]).wait()
    for turn in range(3):
        pltpu.make_async_copy(
            shares.at[turn, pl.ds(0, 3)], shares.at[turn, pl.ds(0, 3)], sends.at[5 + turn]).wait()
    for turn in range(2):
        pltpu.make_async_copy(
            dots.at[turn, pl.ds(0, n_exp - 1)], dots.at[turn, pl.ds(0, n_exp - 1)], sends.at[8 + turn]).wait()


def body(obs_weight, magnitude, star_id, peer_count, zp_index):
    n_sky, n_exp = lax.axis_size("sky"), lax.axis_size("exp")
    blocks = (n_exp, SUB, LANES)
    owned = jax.ShapeDtypeStruct((ZP_PAD, LANES), f32)
    anywhere = pl.BlockSpec(memory_space=pl.ANY)
    inside = pl.BlockSpec(memory_space=pltpu.VMEM)
    x, r = pl.pallas_call(
        functools.partial(kernel, n_sky, n_exp),
        out_shape=(owned, owned),
        in_specs=[pl.BlockSpec(memory_space=pltpu.SMEM)] + [anywhere] * 4,
        out_specs=(inside, inside),
        scratch_shapes=[
            pltpu.VMEM(blocks, f32),
            pltpu.VMEM(blocks, f32),
            pltpu.VMEM(blocks, jnp.int32),
            pltpu.VMEM(blocks, jnp.int32),
            pltpu.VMEM((STAR_ROWS, LANES), f32),
            pltpu.VMEM((STAR_ROWS, LANES), f32),
            pltpu.VMEM((ZP_PAD, LANES), f32),
            pltpu.VMEM((ZP_PAD, LANES), f32),
            pltpu.VMEM((ZP_PAD, LANES), f32),
            pltpu.VMEM((5,) + blocks, f32),
            pltpu.VMEM((5,) + blocks, f32),
            pltpu.VMEM((3, n_sky, ZP_PAD, LANES), f32),
            pltpu.VMEM((2, n_exp, SUB, LANES), f32),
            pltpu.SemaphoreType.DMA((4, SUB)),
            pltpu.SemaphoreType.DMA((10,)),
            pltpu.SemaphoreType.DMA((10, n_exp // PLANE)),
        ],
        compiler_params=pltpu.CompilerParams(collective_id=0, has_side_effects=True),
        name="ubercal_cg",
    )(peer_count, obs_weight, magnitude, star_id, zp_index)
    return x.reshape(-1)[:ZP_DEV], r.reshape(-1)[:ZP_DEV]


def solution(mesh):
    return jax.shard_map(
        body,
        mesh=mesh,
        in_specs=(
            P("sky", "exp", None, None),
            P("sky", "exp", None, None),
            P("sky", "exp", None, None),
            P("sky", "exp", None),
            P("sky", "exp", None, None),
        ),
        out_specs=(P("exp"), P("exp")),
        check_vma=False,
    )
```

time: 476 us -> 79.4 us (0.17)
  matrix products: 304 us -> 0 us
  Pallas kernels: 0 us -> 76.5 us
  waiting for transfers between devices: 42.9 us -> 0 us
  blocking collectives: 38.3 us -> 0 us
  starting transfers between devices: 32.2 us -> 0 us
  local copies, waits for them, and re-layouts: 30.1 us -> 2.06 us
  other arithmetic: 12.6 us -> 0 us
  loops' own time: 7.56 us -> 0 us
  between operations: 6.95 us -> 0.65 us
    dot_general x192 -> x0, matrix products: 304 us -> none  [the longest x112 210 us: sum_one_block(): jnp.einsum('sh,sl->hl', high, low * pair[0][:, None], precision=exact)]
    pallas_call x0 -> x1, Pallas kernels: none -> 76.5 us  [body(): pl.pallas_call(functools.partial(kernel, n_sky, n_exp), out_shape=(owned,...]
    all_to_all x6 -> x0, waiting for transfers between devices: 42.9 us -> none  [the longest x2 15.5 us: slot_values(): lax.all_to_all(picked, 'exp', split_axis=0, concat_axis=0, tiled=True)]
    all_to_all x4 -> x0, blocking collectives: 38.3 us -> none  [the longest x3 27 us: from_everyone(): return lax.all_to_all(copies, axis, split_axis=0, concat_axis=0, tiled=True)]
    all_to_all x6 -> x0, starting transfers between devices: 32.2 us -> none  [the longest x2 13.6 us: reduce_slots(): lax.all_to_all(term, 'exp', split_axis=0, concat_axis=0, tiled=True)]
    dynamic_update_slice x80 -> x0, local copies, waits for them, and re-layouts: 16.4 us -> none  [take_by(): return lax.map(take_one_block, index.reshape(count, block)).reshape(-1)]
    another operation x12 -> x0, loops' own time: 7.56 us -> none  [the longest x7 3.86 us: sum_by(): lax.map(sum_one_block, (values.reshape(count, block), index.reshape(count...]
  transfers between devices with their start and end apart: 6 -> 0, of which waited for: 6 -> 0; matrix products, arithmetic and copies ran while one was open for 0% -> 0% of each run, Pallas kernels for 0% -> 0%
where the time goes in v1:
time: 79.4 us; the launch traced here: 79.2 us
  Pallas kernels  76.5 us (96%)
  local copies, waits for them, and re-layouts  2.06 us (3%)
    pallas_call x1, Pallas kernels, body(): pl.pallas_call(functools.partial(kernel, n_sky, n_exp), out_shape=(owned,...  76.5 us
    unnamed x4, local copies, waits for them, and re-layouts  2.06 us

profile of v1, /device:TPU:1, one launch (start us, length us, event | category | flops | bytes accessed | tf_op | source)
XLA Modules:
  0.0 79.2 jit_solution(11049820734777267596)
XLA Ops:
  0.6 76.5 %ubercal_cg.1 = (f32[96,128]{1,0:T(8,128)}, f32[96,128]{1,0:T(8,128)}) custom-call(s32[1,1,32]{2,1,0:T(1,128)} %count.1, f32[1,1,32,1024]{3,2,1,0:T(8,128)} %weight_in.1, f32[1,1,32,1024]{3,2,1,0:T(8,128)} %magnitude_in.1, s32[1,1,32,1024]{3,2,1,0:T(8,128)} %star_in.1, s32[1,1,32,1024]{3,2,1,0:T(8,128)} %zp_in.1), custom_call_target="tpu_custom_call" | custom-call | tf_op jit(solution)/shard_map/ubercal_cg/pallas_call | solution.py:273
  77.1 0.0 copy-start
  77.1 1.4 %copy.9 = f32[12096]{0:T(1024)} copy(f32[12096]{0:T(1024)} %bitcast.5) | data formatting | bytes 96768
  78.6 0.0 copy-done
  78.6 0.6 copy.10
Async XLA Ops:
  77.1 1.4 %copy-start = (f32[96,128]{1,0:T(8,128)S(1)}, f32[96,128]{1,0:T(8,128)}, u32[]{:S(2)}) copy-start(f32[96,128]{1,0:T(8,128)} %get-tuple-element.5) | copy-start | bytes 147460

commit v2 on v1

v2 whole, which is shorter than its diff:
```python
import functools

import jax
import jax.numpy as jnp
from jax import lax
from jax.experimental import pallas as pl
from jax.experimental.pallas import tpu as pltpu
from jax.sharding import PartitionSpec as P

CAP = 1024
STAR_DEV = 4096
ZP_DEV = 12096
LANES = 128
SUB = CAP // LANES
STAR_ROWS = STAR_DEV // LANES
ZP_ROWS = (ZP_DEV + LANES - 1) // LANES
ZP_PAD = 96
PLANE = 8

OFFSETS = ((0, 0), (0, 1), (0, 3), (1, 0), (3, 0), (1, 1), (0, 2), (2, 0),
           (1, 3), (3, 1), (3, 3), (2, 1), (2, 2), (2, 3), (1, 2), (3, 2))
CHIPS = len(OFFSETS)


def digits(values):
    code = sum(v << (2 * q) for q, v in enumerate(values))
    return code - (1 << 32) if code >= 1 << 31 else code


OFFSET_Z = digits([z for z, _ in OFFSETS])
OFFSET_Y = digits([y for _, y in OFFSETS])

ridge = 1.0
prior = 1.0
f32 = jnp.float32
bf16 = jnp.bfloat16
NT = (((1,), (1,)), ((), ()))
MESH = pl.DeviceIdType.MESH


def two_parts(x):
    coarse = x.astype(bf16)
    return coarse, (x - coarse.astype(f32)).astype(bf16)


def as_code(x):
    return x.astype(f32).astype(bf16)


def row_of(x, r, n):
    return jnp.broadcast_to(x[r : r + 1, :], (n, LANES))


def scatter(high, low, parts, n_high, n_low):
    rows = high.shape[0]
    iota_high = as_code(lax.broadcasted_iota(jnp.int32, (n_high, LANES), 0))
    iota_low = as_code(lax.broadcasted_iota(jnp.int32, (n_low, LANES), 0))
    one, zero = jnp.ones((), bf16), jnp.zeros((), bf16)
    hot, weighted = [], [[] for _ in parts]
    for r in range(rows):
        hot.append(jnp.where(row_of(high, r, n_high) == iota_high, one, zero))
        mask = row_of(low, r, n_low) == iota_low
        for column, part in zip(weighted, parts):
            column.append(jnp.where(mask, row_of(part, r, n_low), zero))
    hot = jnp.concatenate(hot, axis=1)
    weighted = jnp.concatenate([jnp.concatenate(c, axis=1) for c in weighted], axis=0)
    return lax.dot_general(hot, weighted, NT, preferred_element_type=f32)


def pick(table, rows, index):
    high, low = lax.shift_right_logical(index, 7), index & 127
    found = jnp.zeros(index.shape, f32)
    for r in range(rows):
        line = jnp.broadcast_to(table[r : r + 1, :], index.shape)
        found = jnp.where(high == r, jnp.take_along_axis(line, low, axis=1), found)
    return found


def star_codes(index):
    high = lax.shift_right_logical(index, 7) + STAR_ROWS * (lax.shift_right_logical(index, 5) & 3)
    return as_code(high), as_code(index & 31)


def zp_codes(index):
    high = lax.shift_right_logical(index, 7) + ZP_PAD * (lax.shift_right_logical(index, 6) & 1)
    return as_code(high), as_code(index & 63)


def star_table(pair):
    both = pair[:, :32] + pair[:, 32:64]
    return jnp.concatenate([both[32 * q : 32 * q + 32, :] for q in range(4)], axis=1)


def kernel(
    n_sky, n_exp,
    count, weight_in, magnitude_in, star_in, zp_in,
    x_out, r_out,
    weight, magnitude, star, zp, wsum, mean, fields, scale,
    sent, got, shares, dots, loads, sends, arrivals,
):
    sky, me = lax.axis_index("sky"), lax.axis_index("exp")
    my_z, my_y, my_c = me // 8, (me // 2) % 4, me % 2
    partner = 1 - my_c

    def digit(code, q):
        return lax.shift_right_logical(jnp.int32(code), 2 * q) & 3

    def member(q, sign):
        z = (my_z + 4 + sign * digit(OFFSET_Z, q)) & 3
        y = (my_y + 4 + sign * digit(OFFSET_Y, q)) & 3
        return z * 8 + y * 2

    incoming = []
    for a, (source, target) in enumerate(((weight_in, weight), (star_in, star), (magnitude_in, magnitude), (zp_in, zp))):
        for c in range(SUB):
            copy = pltpu.make_async_copy(
                source.at[0, 0, :, pl.ds(c * LANES, LANES)], target.at[:, c, :], loads.at[a, c])
            copy.start()
            incoming.append(copy)

    barrier = pltpu.get_barrier_semaphore()

    @pl.loop(1, n_exp)
    def _(t):
        pl.semaphore_signal(barrier, inc=1, device_id={"exp": lax.rem(me + t, n_exp)}, device_id_type=MESH)

    for t in range(1, n_sky):
        pl.semaphore_signal(barrier, inc=1, device_id={"sky": lax.rem(sky + t, n_sky)}, device_id_type=MESH)

    for copy in incoming[: 3 * SUB]:
        copy.wait()

    slot = lax.broadcasted_iota(jnp.int32, (SUB, LANES), 0) * LANES + lax.broadcasted_iota(jnp.int32, (SUB, LANES), 1)

    def stack(blocks):
        return jnp.concatenate(blocks, axis=0)

    def first(g, total):
        base = g * PLANE
        live = []
        for i in range(PLANE):
            live.append(jnp.where(slot < count[0, 0, base + i], weight[base + i], 0.0))
            weight[base + i] = live[i]
        w = stack(live)
        high, low = star_codes(stack([star[base + i] for i in range(PLANE)]))
        value = w * stack([magnitude[base + i] for i in range(PLANE)])
        return total + scatter(high, low, two_parts(w) + two_parts(value), 128, 32)

    total = lax.fori_loop(0, n_exp // PLANE, first, jnp.zeros((128, 128), f32))
    wsum[...] = prior + star_table(total[:, :64])
    mean[...] = star_table(total[:, 64:]) / wsum[...]

    pl.semaphore_wait(barrier, n_exp - 1 + n_sky - 1)

    def exchange(phase, block, turned):
        @pl.loop(0, CHIPS // 2)
        def _(pair):
            todo = []
            for u in range(2):
                q = CHIPS - 1 - 2 * pair - u if turned else 2 * pair + u
                base = member(q, 1)
                for core in (partner, my_c):
                    j = base + core
                    todo.append((j, q, core is my_c and u == (1 if turned else 0)))
            made = [block(j) for j, _, _ in todo]
            for (j, _, _), x in zip(todo, made):
                sent[phase, j] = x
            for j, q, maybe_own in todo:
                def send(j=j, q=q):
                    pltpu.make_async_remote_copy(
                        src_ref=sent.at[phase, j], dst_ref=got.at[phase, me],
                        send_sem=sends.at[phase], recv_sem=arrivals.at[phase, q // 4],
                        device_id={"exp": j}, device_id_type=MESH).start()

                if maybe_own:
                    pl.when(q != 0)(send)

                    @pl.when(q == 0)
                    def _():
                        pltpu.make_async_copy(sent.at[phase, me], got.at[phase, me], arrivals.at[phase, 0]).start()
                else:
                    send()

    def arrive(phase, group):
        pltpu.make_async_copy(
            sent.at[phase, pl.ds(0, PLANE)], got.at[phase, pl.ds(0, PLANE)], arrivals.at[phase, group]).wait()

    def over_groups(phase, shape, turned, part):
        def one(step, total):
            group = CHIPS // 4 - 1 - step if turned else step
            js = []
            for u in range(4):
                base = member(4 * group + u, -1)
                js += [base, base + 1]
            arrive(phase, group)
            return total + part(js)

        return lax.fori_loop(0, CHIPS // 4, one, jnp.zeros(shape, f32))

    def to_owners(phase, values):
        exchange(phase, lambda j: weight[j] * (values(j) - pick(mean, STAR_ROWS, star[j])), False)

    def star_means(phase):
        def part(js):
            high, low = star_codes(stack([star[j] for j in js]))
            value = stack([weight[j] for j in js]) * stack([got[phase, j] for j in js])
            return scatter(high, low, two_parts(value), 128, 32)

        mean[...] = star_table(over_groups(phase, (128, 64), True, part)) / wsum[...]

    def owner_sums(phase, turn, before_sending=lambda: None):
        def part(js):
            high, low = zp_codes(stack([zp[j] for j in js]))
            return scatter(high, low, two_parts(stack([got[phase, j] for j in js])), 2 * ZP_PAD, 64)

        total = over_groups(phase, (2 * ZP_PAD, LANES), False, part)
        both = total + pltpu.roll(total, 64, 1)
        lane = lax.broadcasted_iota(jnp.int32, (ZP_PAD, LANES), 1)
        shares[turn, sky, pl.ds(0, ZP_PAD)] = jnp.where(lane < 64, both[:ZP_PAD], both[ZP_PAD:])
        before_sending()
        for t in (2, 1, 3):
            pltpu.make_async_remote_copy(
                src_ref=shares.at[turn, sky], dst_ref=shares.at[turn, sky],
                send_sem=sends.at[5 + turn], recv_sem=arrivals.at[5 + turn, 0],
                device_id={"sky": lax.rem(sky + t, n_sky)}, device_id_type=MESH).start()
        pltpu.make_async_copy(
            shares.at[turn, pl.ds(0, 3)], shares.at[turn, pl.ds(0, 3)], arrivals.at[5 + turn, 0]).wait()
        part = [shares[turn, i, pl.ds(0, ZP_PAD)] for i in range(4)]
        return (part[0] + part[1]) + (part[2] + part[3])

    def put_dots(turn, rows):
        dots[turn, me] = stack(rows + [jnp.zeros((1, LANES), f32)] * (SUB - len(rows)))

        @pl.loop(1, n_exp)
        def _(t):
            pltpu.make_async_remote_copy(
                src_ref=dots.at[turn, me], dst_ref=dots.at[turn, me],
                send_sem=sends.at[8 + turn], recv_sem=arrivals.at[8 + turn, 0],
                device_id={"exp": lax.rem(me + t, n_exp)}, device_id_type=MESH).start()

    def take_dots(turn):
        pltpu.make_async_copy(
            dots.at[turn, pl.ds(0, n_exp - 1)], dots.at[turn, pl.ds(0, n_exp - 1)], arrivals.at[8 + turn, 0]).wait()
        return jnp.sum(dots[turn], axis=0)

    def column(x):
        return jnp.sum(x, axis=0, keepdims=True)

    to_owners(0, lambda j: magnitude[j])
    for copy in incoming[3 * SUB :]:
        copy.wait()
    for turn in range(3):
        shares[turn, sky, pl.ds(ZP_PAD, SUB)] = jnp.zeros((SUB, LANES), f32)
    fields[0] = owner_sums(0, 0)

    @pl.loop(0, 2)
    def _(turn):
        taken, given = 2 * turn + 1, 2 * turn + 2
        exchange(taken, lambda k: pick(fields.at[turn], ZP_ROWS, zp[k]), True)

        @pl.when(turn == 1)
        def _():
            b, c = fields[0], fields[1]
            put_dots(0, [column(b * b), column(b * c)])

        star_means(taken)
        to_owners(given, lambda j: got[taken, j])

        @pl.when(turn == 1)
        def _():
            sums = jnp.sum(take_dots(0), axis=1, keepdims=True)
            alpha = jnp.broadcast_to(sums[0:1] / sums[1:2], (1, LANES))
            scale[0:1] = alpha
            scale[1:2] = jnp.broadcast_to(sums[0:1], (1, LANES))
            b, c = fields[0], fields[1]
            r = b - alpha * c
            slots = [jnp.zeros((SUB, LANES), f32)] * 3

            def add(j, slots):
                v, t = got[1, j], sent[2, j]
                w, s = v - alpha * got[3, j], t - alpha * sent[4, j]
                return [slots[0] + w * s, slots[1] + v * s, slots[2] + v * t]

            slots = lax.fori_loop(0, n_exp, add, slots, unroll=4)
            put_dots(1, [column(x) for x in slots] + [column(r * r), column(r * b)])

        def with_dots():
            @pl.when(turn == 1)
            def _():
                shares[2, sky, pl.ds(ZP_PAD, SUB)] = take_dots(1)

        fields[turn + 1] = owner_sums(given, turn + 1, with_dots) + ridge * fields[turn]

    b, c, d = fields[0], fields[1], fields[2]
    alpha, norm_now = scale[0:1], scale[1:2]
    last = [shares[2, i, pl.ds(ZP_PAD, SUB)] for i in range(4)]
    sums = jnp.broadcast_to(jnp.sum((last[0] + last[1]) + (last[2] + last[3]), axis=1, keepdims=True), (SUB, LANES))
    norm_next, cross = 0.25 * sums[3:4], 0.25 * sums[4:5]
    ratio = norm_next / norm_now
    square = norm_next + 2.0 * ratio * cross + ratio * ratio * norm_now
    curve = ridge * square + (sums[0:1] + 2.0 * ratio * sums[1:2] + ratio * ratio * sums[2:3])
    step = norm_next / curve
    r = b - alpha * c
    x_out[...] = alpha * b + step * (r + ratio * b)
    r_out[...] = r - step * ((c - alpha * d) + ratio * c)

    for phase in range(5):
        pltpu.make_async_copy(
            sent.at[phase, pl.ds(0, n_exp - 1)], got.at[phase, pl.ds(0, n_exp - 1)], sends.at[phase]).wait()
    for turn in range(3):
        pltpu.make_async_copy(
            shares.at[turn, pl.ds(0, 3)], shares.at[turn, pl.ds(0, 3)], sends.at[5 + turn]).wait()
    for turn in range(2):
        pltpu.make_async_copy(
            dots.at[turn, pl.ds(0, n_exp - 1)], dots.at[turn, pl.ds(0, n_exp - 1)], sends.at[8 + turn]).wait()


def body(obs_weight, magnitude, star_id, peer_count, zp_index):
    n_sky, n_exp = lax.axis_size("sky"), lax.axis_size("exp")
    blocks = (n_exp, SUB, LANES)
    owned = jax.ShapeDtypeStruct((ZP_PAD, LANES), f32)
    anywhere = pl.BlockSpec(memory_space=pl.ANY)
    inside = pl.BlockSpec(memory_space=pltpu.VMEM)
    x, r = pl.pallas_call(
        functools.partial(kernel, n_sky, n_exp),
        out_shape=(owned, owned),
        in_specs=[pl.BlockSpec(memory_space=pltpu.SMEM)] + [anywhere] * 4,
        out_specs=(inside, inside),
        scratch_shapes=[
            pltpu.VMEM(blocks, f32),
            pltpu.VMEM(blocks, f32),
            pltpu.VMEM(blocks, jnp.int32),
            pltpu.VMEM(blocks, jnp.int32),
            pltpu.VMEM((STAR_ROWS, LANES), f32),
            pltpu.VMEM((STAR_ROWS, LANES), f32),
            pltpu.VMEM((3, ZP_PAD, LANES), f32),
            pltpu.VMEM((SUB, LANES), f32),
            pltpu.VMEM((5,) + blocks, f32),
            pltpu.VMEM((5,) + blocks, f32),
            pltpu.VMEM((3, n_sky, ZP_PAD + SUB, LANES), f32),
            pltpu.VMEM((2, n_exp, SUB, LANES), f32),
            pltpu.SemaphoreType.DMA((4, SUB)),
            pltpu.SemaphoreType.DMA((10,)),
            pltpu.SemaphoreType.DMA((10, CHIPS // 4)),
        ],
        compiler_params=pltpu.CompilerParams(collective_id=0, has_side_effects=True),
        name="ubercal_cg",
    )(peer_count, obs_weight, magnitude, star_id, zp_index)
    return x.reshape(-1)[:ZP_DEV], r.reshape(-1)[:ZP_DEV]


def solution(mesh):
    return jax.shard_map(
        body,
        mesh=mesh,
        in_specs=(
            P("sky", "exp", None, None),
            P("sky", "exp", None, None),
            P("sky", "exp", None, None),
            P("sky", "exp", None),
            P("sky", "exp", None, None),
        ),
        out_specs=(P("exp"), P("exp")),
        check_vma=False,
    )
```

time: 79.4 us -> 70.7 us (0.89)
  Pallas kernels: 76.5 us -> 67.7 us
    pallas_call x1, Pallas kernels: 76.5 us -> 67.7 us  [body(): pl.pallas_call(functools.partial(kernel, n_sky, n_exp), out_shape=(owned,...]
where the time goes in v2:
time: 70.7 us; the launch traced here: 70.4 us
  Pallas kernels  67.7 us (96%)
  local copies, waits for them, and re-layouts  2.06 us (3%)
    pallas_call x1, Pallas kernels, body(): pl.pallas_call(functools.partial(kernel, n_sky, n_exp), out_shape=(owned,...  67.7 us
    unnamed x4, local copies, waits for them, and re-layouts  2.06 us

profile of v2, /device:TPU:1, one launch (start us, length us, event | category | flops | bytes accessed | tf_op | source)
XLA Modules:
  0.0 70.4 jit_solution(18052051231713837835)
XLA Ops:
  0.6 67.7 %ubercal_cg.1 = (f32[96,128]{1,0:T(8,128)}, f32[96,128]{1,0:T(8,128)}) custom-call(s32[1,1,32]{2,1,0:T(1,128)} %count.1, f32[1,1,32,1024]{3,2,1,0:T(8,128)} %weight_in.1, f32[1,1,32,1024]{3,2,1,0:T(8,128)} %magnitude_in.1, s32[1,1,32,1024]{3,2,1,0:T(8,128)} %star_in.1, s32[1,1,32,1024]{3,2,1,0:T(8,128)} %zp_in.1), custom_call_target="tpu_custom_call" | custom-call | tf_op jit(solution)/shard_map/ubercal_cg/pallas_call | solution.py:324
  68.4 0.0 copy-start
  68.4 1.4 %copy.9 = f32[12096]{0:T(1024)} copy(f32[12096]{0:T(1024)} %bitcast.5) | data formatting | bytes 96768
  69.8 0.0 copy-done
  69.8 0.6 copy.10
Async XLA Ops:
  68.4 1.4 %copy-start = (f32[96,128]{1,0:T(8,128)S(1)}, f32[96,128]{1,0:T(8,128)}, u32[]{:S(2)}) copy-start(f32[96,128]{1,0:T(8,128)} %get-tuple-element.5) | copy-start | bytes 147460

commit v3 on v2

--- a/solution.py
+++ b/solution.py
@@ -318,7 +318,7 @@
 def body(obs_weight, magnitude, star_id, peer_count, zp_index):
     n_sky, n_exp = lax.axis_size("sky"), lax.axis_size("exp")
     blocks = (n_exp, SUB, LANES)
-    owned = jax.ShapeDtypeStruct((ZP_PAD, LANES), f32)
+    owned = pltpu.VMEM((ZP_PAD, LANES), f32)
     anywhere = pl.BlockSpec(memory_space=pl.ANY)
     inside = pl.BlockSpec(memory_space=pltpu.VMEM)
     x, r = pl.pallas_call(

time: 70.7 us -> 69.2 us (0.979)
  local copies, waits for them, and re-layouts: 2.06 us -> 1.25 us
    unnamed x4 -> x2, local copies, waits for them, and re-layouts: 2.06 us -> 1.25 us
where the time goes in v3:
time: 69.2 us; the launch traced here: 69 us
  Pallas kernels  67.1 us (97%)
  local copies, waits for them, and re-layouts  1.25 us (2%)
    pallas_call x1, Pallas kernels, body(): pl.pallas_call(functools.partial(kernel, n_sky, n_exp), out_shape=(owned,...  67.1 us

profile of v3, /device:TPU:1, one launch (start us, length us, event | category | flops | bytes accessed | tf_op | source)
XLA Modules:
  0.0 69.0 jit_solution(12294963247886128154)
XLA Ops:
  0.6 67.1 %ubercal_cg.1 = (f32[96,128]{1,0:T(8,128)S(1)}, f32[96,128]{1,0:T(8,128)S(1)}) custom-call(s32[1,1,32]{2,1,0:T(1,128)} %count.1, f32[1,1,32,1024]{3,2,1,0:T(8,128)} %weight_in.1, f32[1,1,32,1024]{3,2,1,0:T(8,128)} %magnitude_in.1, s32[1,1,32,1024]{3,2,1,0:T(8,128)} %star_in.1, s32[1,1,32,1024]{3,2,1,0:T(8,128)} %zp_in.1), custom_call_target="tpu_custom_call" | custom-call | tf_op jit(solution)/shard_map/ubercal_cg/pallas_call | solution.py:324
  67.7 0.6 copy.9
  68.4 0.6 copy.10

commit v4 on v3

--- a/solution.py
+++ b/solution.py
@@ -94,7 +94,7 @@
 def kernel(
     n_sky, n_exp,
     count, weight_in, magnitude_in, star_in, zp_in,
-    x_out, r_out,
+    out,
     weight, magnitude, star, zp, wsum, mean, fields, scale,
     sent, got, shares, dots, loads, sends, arrivals,
 ):
@@ -301,8 +301,8 @@
     curve = ridge * square + (sums[0:1] + 2.0 * ratio * sums[1:2] + ratio * ratio * sums[2:3])
     step = norm_next / curve
     r = b - alpha * c
-    x_out[...] = alpha * b + step * (r + ratio * b)
-    r_out[...] = r - step * ((c - alpha * d) + ratio * c)
+    out[0] = alpha * b + step * (r + ratio * b)
+    out[1] = r - step * ((c - alpha * d) + ratio * c)
 
     for phase in range(5):
         pltpu.make_async_copy(
@@ -318,14 +318,14 @@
 def body(obs_weight, magnitude, star_id, peer_count, zp_index):
     n_sky, n_exp = lax.axis_size("sky"), lax.axis_size("exp")
     blocks = (n_exp, SUB, LANES)
-    owned = pltpu.VMEM((ZP_PAD, LANES), f32)
+    owned = pltpu.VMEM((2, ZP_PAD, LANES), f32)
     anywhere = pl.BlockSpec(memory_space=pl.ANY)
     inside = pl.BlockSpec(memory_space=pltpu.VMEM)
-    x, r = pl.pallas_call(
+    both = pl.pallas_call(
         functools.partial(kernel, n_sky, n_exp),
-        out_shape=(owned, owned),
+        out_shape=owned,
         in_specs=[pl.BlockSpec(memory_space=pltpu.SMEM)] + [anywhere] * 4,
-        out_specs=(inside, inside),
+        out_specs=inside,
         scratch_shapes=[
             pltpu.VMEM(blocks, f32),
             pltpu.VMEM(blocks, f32),
@@ -346,7 +346,7 @@
         compiler_params=pltpu.CompilerParams(collective_id=0, has_side_effects=True),
         name="ubercal_cg",
     )(peer_count, obs_weight, magnitude, star_id, zp_index)
-    return x.reshape(-1)[:ZP_DEV], r.reshape(-1)[:ZP_DEV]
+    return both[0].reshape(-1)[:ZP_DEV], both[1].reshape(-1)[:ZP_DEV]
 
 
 def solution(mesh):

time: 69.2 us -> 68.2 us (0.986)
    unnamed x2 -> x0, local copies, waits for them, and re-layouts: 1.25 us -> none
where the time goes in v4:
time: 68.2 us; the launch traced here: 68 us
  Pallas kernels  66.7 us (98%)
    pallas_call x1, Pallas kernels, body(): pl.pallas_call(functools.partial(kernel, n_sky, n_exp), out_shape=owned,...  66.7 us

profile of v4, /device:TPU:1, one launch (start us, length us, event | category | flops | bytes accessed | tf_op | source)
XLA Modules:
  0.0 68.0 jit_solution(15399025733261243022)
XLA Ops:
  0.6 66.7 %ubercal_cg.1 = f32[2,96,128]{2,1,0:T(8,128)S(1)} custom-call(s32[1,1,32]{2,1,0:T(1,128)} %count.1, f32[1,1,32,1024]{3,2,1,0:T(8,128)} %weight_in.1, f32[1,1,32,1024]{3,2,1,0:T(8,128)} %magnitude_in.1, s32[1,1,32,1024]{3,2,1,0:T(8,128)} %star_in.1, s32[1,1,32,1024]{3,2,1,0:T(8,128)} %zp_in.1), custom_call_target="tpu_custom_call" | custom-call | tf_op jit(solution)/shard_map/ubercal_cg/pallas_call | solution.py:324
  67.3 0.6 slice_bitcast_fusion

commit v5 on v4

--- a/solution.py
+++ b/solution.py
@@ -136,17 +136,17 @@
         return jnp.concatenate(blocks, axis=0)
 
     def first(g, total):
-        base = g * PLANE
+        base = g * (2 * PLANE)
         live = []
-        for i in range(PLANE):
+        for i in range(2 * PLANE):
             live.append(jnp.where(slot < count[0, 0, base + i], weight[base + i], 0.0))
             weight[base + i] = live[i]
         w = stack(live)
-        high, low = star_codes(stack([star[base + i] for i in range(PLANE)]))
-        value = w * stack([magnitude[base + i] for i in range(PLANE)])
+        high, low = star_codes(stack([star[base + i] for i in range(2 * PLANE)]))
+        value = w * stack([magnitude[base + i] for i in range(2 * PLANE)])
         return total + scatter(high, low, two_parts(w) + two_parts(value), 128, 32)
 
-    total = lax.fori_loop(0, n_exp // PLANE, first, jnp.zeros((128, 128), f32))
+    total = lax.fori_loop(0, n_exp // (2 * PLANE), first, jnp.zeros((128, 128), f32))
     wsum[...] = prior + star_table(total[:, :64])
     mean[...] = star_table(total[:, 64:]) / wsum[...]
 
@@ -216,7 +216,7 @@
         total = over_groups(phase, (2 * ZP_PAD, LANES), False, part)
         both = total + pltpu.roll(total, 64, 1)
         lane = lax.broadcasted_iota(jnp.int32, (ZP_PAD, LANES), 1)
-        shares[turn, sky, pl.ds(0, ZP_PAD)] = jnp.where(lane < 64, both[:ZP_PAD], both[ZP_PAD:])
+        shares[turn, sky] = jnp.where(lane < 64, both[:ZP_PAD], both[ZP_PAD:])
         before_sending()
         for t in (2, 1, 3):
             pltpu.make_async_remote_copy(
@@ -225,7 +225,7 @@
                 device_id={"sky": lax.rem(sky + t, n_sky)}, device_id_type=MESH).start()
         pltpu.make_async_copy(
             shares.at[turn, pl.ds(0, 3)], shares.at[turn, pl.ds(0, 3)], arrivals.at[5 + turn, 0]).wait()
-        part = [shares[turn, i, pl.ds(0, ZP_PAD)] for i in range(4)]
+        part = [shares[turn, i] for i in range(4)]
         return (part[0] + part[1]) + (part[2] + part[3])
 
     def put_dots(turn, rows):
@@ -246,11 +246,12 @@
     def column(x):
         return jnp.sum(x, axis=0, keepdims=True)
 
+    diagonal = (lax.broadcasted_iota(jnp.int32, (SUB, LANES), 0)
+                == lax.broadcasted_iota(jnp.int32, (SUB, LANES), 1))
+
     to_owners(0, lambda j: magnitude[j])
     for copy in incoming[3 * SUB :]:
         copy.wait()
-    for turn in range(3):
-        shares[turn, sky, pl.ds(ZP_PAD, SUB)] = jnp.zeros((SUB, LANES), f32)
     fields[0] = owner_sums(0, 0)
 
     @pl.loop(0, 2)
@@ -287,14 +288,15 @@
         def with_dots():
             @pl.when(turn == 1)
             def _():
-                shares[2, sky, pl.ds(ZP_PAD, SUB)] = take_dots(1)
+                sums = jnp.sum(take_dots(1), axis=1, keepdims=True)
+                shares[2, sky, pl.ds(ZP_PAD - 1, 1)] = column(jnp.where(diagonal, sums, 0.0))
 
         fields[turn + 1] = owner_sums(given, turn + 1, with_dots) + ridge * fields[turn]
 
     b, c, d = fields[0], fields[1], fields[2]
     alpha, norm_now = scale[0:1], scale[1:2]
-    last = [shares[2, i, pl.ds(ZP_PAD, SUB)] for i in range(4)]
-    sums = jnp.broadcast_to(jnp.sum((last[0] + last[1]) + (last[2] + last[3]), axis=1, keepdims=True), (SUB, LANES))
+    sums = jnp.sum(jnp.where(diagonal, d[ZP_PAD - 1 :], 0.0), axis=1, keepdims=True)
+    sums = jnp.broadcast_to(sums, (SUB, LANES))
     norm_next, cross = 0.25 * sums[3:4], 0.25 * sums[4:5]
     ratio = norm_next / norm_now
     square = norm_next + 2.0 * ratio * cross + ratio * ratio * norm_now
@@ -337,7 +339,7 @@
             pltpu.VMEM((SUB, LANES), f32),
             pltpu.VMEM((5,) + blocks, f32),
             pltpu.VMEM((5,) + blocks, f32),
-            pltpu.VMEM((3, n_sky, ZP_PAD + SUB, LANES), f32),
+            pltpu.VMEM((3, n_sky, ZP_PAD, LANES), f32),
             pltpu.VMEM((2, n_exp, SUB, LANES), f32),
             pltpu.SemaphoreType.DMA((4, SUB)),
             pltpu.SemaphoreType.DMA((10,)),

time: 68.2 us -> 67.8 us (level)
  no operation moved by 1% of the time
where the time goes in v5:
time: 67.8 us; the launch traced here: 67.6 us
  Pallas kernels  66.3 us (98%)
    pallas_call x1, Pallas kernels, body(): pl.pallas_call(functools.partial(kernel, n_sky, n_exp), out_shape=owned,...  66.3 us

profile of v5, /device:TPU:1, one launch (start us, length us, event | category | flops | bytes accessed | tf_op | source)
XLA Modules:
  0.0 67.6 jit_solution(5140480256914808841)
XLA Ops:
  0.6 66.3 %ubercal_cg.1 = f32[2,96,128]{2,1,0:T(8,128)S(1)} custom-call(s32[1,1,32]{2,1,0:T(1,128)} %count.1, f32[1,1,32,1024]{3,2,1,0:T(8,128)} %weight_in.1, f32[1,1,32,1024]{3,2,1,0:T(8,128)} %magnitude_in.1, s32[1,1,32,1024]{3,2,1,0:T(8,128)} %star_in.1, s32[1,1,32,1024]{3,2,1,0:T(8,128)} %zp_in.1), custom_call_target="tpu_custom_call" | custom-call | tf_op jit(solution)/shard_map/ubercal_cg/pallas_call | solution.py:326
  66.9 0.6 slice_bitcast_fusion

commit v6 on v5

--- a/solution.py
+++ b/solution.py
@@ -228,20 +228,22 @@
         part = [shares[turn, i] for i in range(4)]
         return (part[0] + part[1]) + (part[2] + part[3])
 
+    sizes = (2, SUB)
+
     def put_dots(turn, rows):
         dots[turn, me] = stack(rows + [jnp.zeros((1, LANES), f32)] * (SUB - len(rows)))
 
         @pl.loop(1, n_exp)
         def _(t):
             pltpu.make_async_remote_copy(
-                src_ref=dots.at[turn, me], dst_ref=dots.at[turn, me],
+                src_ref=dots.at[turn, me, pl.ds(0, sizes[turn])], dst_ref=dots.at[turn, me, pl.ds(0, sizes[turn])],
                 send_sem=sends.at[8 + turn], recv_sem=arrivals.at[8 + turn, 0],
                 device_id={"exp": lax.rem(me + t, n_exp)}, device_id_type=MESH).start()
 
     def take_dots(turn):
         pltpu.make_async_copy(
-            dots.at[turn, pl.ds(0, n_exp - 1)], dots.at[turn, pl.ds(0, n_exp - 1)], arrivals.at[8 + turn, 0]).wait()
-        return jnp.sum(dots[turn], axis=0)
+            dots.at[turn, pl.ds(0, n_exp - 1), pl.ds(0, sizes[turn])], dots.at[turn, pl.ds(0, n_exp - 1), pl.ds(0, sizes[turn])], arrivals.at[8 + turn, 0]).wait()
+        return jnp.sum(dots[turn, :, pl.ds(0, sizes[turn])], axis=0)
 
     def column(x):
         return jnp.sum(x, axis=0, keepdims=True)
@@ -314,7 +316,7 @@
             shares.at[turn, pl.ds(0, 3)], shares.at[turn, pl.ds(0, 3)], sends.at[5 + turn]).wait()
     for turn in range(2):
         pltpu.make_async_copy(
-            dots.at[turn, pl.ds(0, n_exp - 1)], dots.at[turn, pl.ds(0, n_exp - 1)], sends.at[8 + turn]).wait()
+            dots.at[turn, pl.ds(0, n_exp - 1), pl.ds(0, sizes[turn])], dots.at[turn, pl.ds(0, n_exp - 1), pl.ds(0, sizes[turn])], sends.at[8 + turn]).wait()
 
 
 def body(obs_weight, magnitude, star_id, peer_count, zp_index):

time: 67.8 us -> 67.8 us (level)
  no operation moved by 1% of the time
where the time goes in v6:
time: 67.8 us; the launch traced here: 67.6 us
  Pallas kernels  66.3 us (98%)
    pallas_call x1, Pallas kernels, body(): pl.pallas_call(functools.partial(kernel, n_sky, n_exp), out_shape=owned,...  66.3 us

profile of v6, /device:TPU:1, one launch (start us, length us, event | category | flops | bytes accessed | tf_op | source)
XLA Modules:
  0.0 67.6 jit_solution(14762873972101011944)
XLA Ops:
  0.6 66.3 %ubercal_cg.1 = f32[2,96,128]{2,1,0:T(8,128)S(1)} custom-call(s32[1,1,32]{2,1,0:T(1,128)} %count.1, f32[1,1,32,1024]{3,2,1,0:T(8,128)} %weight_in.1, f32[1,1,32,1024]{3,2,1,0:T(8,128)} %magnitude_in.1, s32[1,1,32,1024]{3,2,1,0:T(8,128)} %star_in.1, s32[1,1,32,1024]{3,2,1,0:T(8,128)} %zp_in.1), custom_call_target="tpu_custom_call" | custom-call | tf_op jit(solution)/shard_map/ubercal_cg/pallas_call | solution.py:328
  66.9 0.6 slice_bitcast_fusion
